TPU v7x, 32 devices: a whole 2x2x4 slice. The times are simulated.
32 devices in a mesh: ctx: 4 (over y, x), vis: 8 (over z, core).
Axes of the slice: x: 2, y: 2, z: 4, core: 2. Of those that a mesh axis runs over, the one named last changes fastest.
Arguments:
- patches: bfloat16 [4096, 1280], P(('ctx', 'vis')), may hold values from -10 to 10
- vis_gain: float32 [1280], replicated, may hold values from 0.5 to 1.5
- w_qkv: bfloat16 [1280, 3840], P(None, 'vis'), may hold values from -2 to 2
- w_out: bfloat16 [1280, 1280], P('vis'), may hold values from -0.15625 to 0.15625
- merge_gain: float32 [1280], replicated, may hold values from 0.5 to 1.5
- w_merge: bfloat16 [5120, 8192], P(None, 'vis'), may hold values from -0.078125 to 0.078125
- token_dest: int32 [4, 256], replicated, may hold values from 0 to 3, as said below
- token_row: int32 [4, 256], replicated, may hold values from 0 to 1023, as said below
- prompt_text: bfloat16 [4096, 8192], P('ctx', 'vis'), may hold values from -6 to 6
- kv_gain: float32 [8192], P('vis'), may hold values from 0.5 to 1.5
- w_kv: bfloat16 [8192, 1024], P('vis'), may hold values from -1 to 1
- queries: bfloat16 [512, 4096], P('ctx'), may hold values from -12 to 12
- resp_kv: bfloat16 [512, 1024], P('ctx'), may hold values from -12 to 12
- resp_len: int32 [4], P('ctx'), may hold values from 64 to 128
Outputs:
- attended: bfloat16 [512, 4096], P('ctx')
Inputs may be any that keep to these rules, and one draw needn't show every extreme that they name: `token_dest`: the tokens of one image are in order of their prompt shard; at most 96 tokens of one image go to one shard, and from every image exactly 96 go to some shard. `token_row`: no two visual tokens take the same position of one shard.
All inputs are finite; a program needn't handle non-finite values.
Results may differ from a plain program's by a relative error of at most 0.014.
Values may be sent and summed in bfloat16 or wider, within the bound.
A program may use at most 128 MiB of HBM per device.

v0:
```python
import math
import jax
import jax.numpy as jnp
from jax import lax
from jax.sharding import PartitionSpec as P

VD = 1280
VHEADS = 16
D = 8192
HD = 128
QH = 32
KVH = 4
VHD = 80
MD = 5120
EPS = 1e-06


def merged_2(shard, axis, combine):
    everything = jax.tree.map(lambda part: lax.all_gather(part, axis), shard)
    initial = jax.tree.map(lambda part: part[0], everything)

    def lap(k, so_far):
        return combine(so_far, jax.tree.map(lambda part: part[k], everything))

    return lax.fori_loop(1, lax.axis_size(axis), lap, initial)


def layer_norm(values, gain):
    center = values - jnp.mean(values, axis=-1, keepdims=True)
    spread = jnp.mean(center * center, axis=-1, keepdims=True)
    return center * lax.rsqrt(spread + EPS) * gain


def dense_attention(query, keys, values):
    count = query.shape[0]
    block = min(512, count)
    scale = 1.0 / math.sqrt(query.shape[1])

    def one_block(part):
        scores = jnp.dot(part, keys.T, preferred_element_type=jnp.float32) * scale
        highest = jnp.max(scores, axis=1, keepdims=True)
        expo = jnp.exp(scores - highest)
        summed = jnp.sum(expo, axis=1, keepdims=True)
        mixed = jnp.dot(expo.astype(jnp.bfloat16), values, preferred_element_type=jnp.float32)
        return (mixed / summed).astype(jnp.bfloat16)

    blocks = query.reshape(count // block, block, query.shape[1])
    return lax.map(one_block, blocks).reshape(count, values.shape[1])


def head_attention(packed):
    stacked = jnp.transpose(packed, (1, 0, 2))

    def one_head(item):
        return dense_attention(item[:, :VHD], item[:, VHD : 2 * VHD], item[:, 2 * VHD :])

    return jnp.transpose(lax.map(one_head, stacked), (1, 0, 2))


def combine_partial(first, second):
    highest = jnp.maximum(first[0], second[0])
    fade_one = jnp.exp(first[0] - highest)
    fade_two = jnp.exp(second[0] - highest)
    return (
        highest,
        first[1] * fade_one + second[1] * fade_two,
        first[2] * fade_one[..., None] + second[2] * fade_two[..., None],
    )


def per_device(
    patches,
    vis_gain,
    w_qkv,
    w_out,
    merge_gain,
    w_merge,
    token_dest,
    token_row,
    prompt_text,
    kv_gain,
    w_kv,
    queries,
    resp_kv,
    resp_len,
):
    ctx_count = lax.axis_size("ctx")
    vis_count = lax.axis_size("vis")
    ctx_index = lax.axis_index("ctx")
    vis_index = lax.axis_index("vis")
    patch_count = patches.shape[0]
    floats = patches.astype(jnp.float32)
    normed = layer_norm(floats, vis_gain).astype(jnp.bfloat16)
    local_heads = VHEADS // vis_count
    qkv = jnp.dot(
        lax.all_gather(normed, "vis", axis=0, tiled=True), w_qkv, preferred_element_type=jnp.float32
    ).astype(jnp.bfloat16)
    image_rows = qkv.shape[0]
    heads = head_attention(qkv.reshape(image_rows, local_heads, 3 * VHD))
    returned = lax.all_to_all(heads, "vis", split_axis=0, concat_axis=1, tiled=True).reshape(
        patch_count, VD
    )
    projected = jnp.dot(
        returned,
        lax.all_gather(w_out, "vis", axis=0, tiled=True),
        preferred_element_type=jnp.float32,
    )
    mixed = floats + projected
    merged = layer_norm(mixed, merge_gain).astype(jnp.bfloat16).reshape(patch_count // 4, MD)
    visual = jnp.dot(
        lax.all_gather(merged, "vis", axis=0, tiled=True),
        w_merge,
        preferred_element_type=jnp.float32,
    ).astype(jnp.bfloat16)
    image_tokens = visual.shape[0]
    capacity = 3 * (image_tokens // ctx_count) // 2
    slots = jnp.arange(capacity, dtype=jnp.int32)
    shard_rows = prompt_text.shape[0]
    own_dest = lax.dynamic_index_in_dim(token_dest, ctx_index, 0, keepdims=False)
    shards = jnp.arange(ctx_count, dtype=jnp.int32)
    counts_out = jnp.sum((own_dest[None, :] == shards[:, None]).astype(jnp.int32), axis=1)
    starts_out = jnp.cumsum(counts_out) - counts_out
    picks = jnp.clip(starts_out[:, None] + slots[None, :], 0, image_tokens - 1).reshape(-1)
    filled = (slots[None, :] < counts_out[:, None]).reshape(-1, 1)
    outgoing = jnp.take(visual, picks, axis=0)
    outgoing = jnp.where(filled, outgoing, jnp.zeros_like(outgoing)).reshape(
        ctx_count, capacity, -1
    )
    arrived = lax.all_to_all(outgoing, "ctx", split_axis=0, concat_axis=0, tiled=True)
    pool = arrived.reshape(ctx_count * capacity, -1)
    firsts = jnp.sum((token_dest < ctx_index).astype(jnp.int32), axis=1)
    counts_in = jnp.sum((token_dest == ctx_index).astype(jnp.int32), axis=1)
    lookup = jnp.clip(firsts[:, None] + slots[None, :], 0, image_tokens - 1)
    places = jnp.take_along_axis(token_row, lookup, axis=1)
    live = slots[None, :] < counts_in[:, None]
    targets = jnp.where(live, places, shard_rows).reshape(-1)
    numbers = jnp.arange(ctx_count * capacity, dtype=jnp.int32) + 1
    source = jnp.zeros((shard_rows,), jnp.int32).at[targets].set(numbers, mode="drop")
    incoming = jnp.take(pool, jnp.maximum(source - 1, 0), axis=0)
    prompt = jnp.where((source > 0)[:, None], incoming, prompt_text)
    prompt_floats = prompt.astype(jnp.float32)
    squares = lax.psum(jnp.sum(prompt_floats * prompt_floats, axis=1), "vis")
    inverse = lax.rsqrt(squares / D + EPS)
    scaled = (prompt_floats * inverse[:, None] * kv_gain).astype(jnp.bfloat16)
    kv_share = lax.psum_scatter(
        jnp.dot(scaled, w_kv, preferred_element_type=jnp.float32),
        "vis",
        scatter_dimension=0,
        tiled=True,
    ).astype(jnp.bfloat16)
    width = KVH * HD
    group = QH // KVH
    resp_rows = queries.shape[0]
    scale = 1.0 / math.sqrt(HD)
    q_heads = queries.reshape(resp_rows, KVH, group, HD)

    def update(state, keys, values, visible):
        highest, summed, weighted = state
        scores = (
            jnp.einsum("rkgd,nkd->kgrn", q_heads, keys, preferred_element_type=jnp.float32) * scale
        )
        if visible is not None:
            scores = jnp.where(visible, scores, -1e30)
        new_high = jnp.maximum(highest, jnp.max(scores, axis=3))
        expo = jnp.exp(scores - new_high[..., None])
        if visible is not None:
            expo = jnp.where(visible, expo, 0.0)
        fade = jnp.exp(highest - new_high)
        summed = summed * fade + jnp.sum(expo, axis=3)
        weighted = weighted * fade[..., None] + jnp.einsum(
            "kgrn,nkd->kgrd", expo.astype(jnp.bfloat16), values, preferred_element_type=jnp.float32
        )
        return (new_high, summed, weighted)

    def fold_block(state, piece):
        count = piece.shape[0]
        return update(
            state,
            piece[:, :width].reshape(count, KVH, HD),
            piece[:, width:].reshape(count, KVH, HD),
            None,
        )

    def fold_prompt(state, piece):
        count = piece.shape[0]
        if count > 512 and count % 512 == 0:
            blocks = piece.reshape(count // 512, 512, 2 * width)

            def scan_step(inner, block):
                return (fold_block(inner, block), None)

            state, unused = lax.scan(scan_step, state, blocks)
            return state
        return fold_block(state, piece)

    own_count = resp_rows // vis_count
    own = lax.dynamic_slice_in_dim(resp_kv, vis_index * own_count, own_count, 0)
    key_positions = vis_index * own_count + jnp.arange(own_count, dtype=jnp.int32)
    query_positions = jnp.arange(resp_rows, dtype=jnp.int32)
    own_visible = key_positions[None, :] <= query_positions[:, None]
    start_state = (
        jnp.full((KVH, group, resp_rows), -1e30, jnp.float32),
        jnp.zeros((KVH, group, resp_rows), jnp.float32),
        jnp.zeros((KVH, group, resp_rows, HD), jnp.float32),
    )
    state = update(
        start_state,
        own[:, :width].reshape(own_count, KVH, HD),
        own[:, width:].reshape(own_count, KVH, HD),
        own_visible,
    )
    state = fold_prompt(state, lax.all_gather(kv_share, "ctx", axis=0, tiled=True))
    highest, summed, weighted = merged_2(state, "vis", combine_partial)
    result = weighted / summed[..., None]
    result = jnp.transpose(result, (2, 0, 1, 3)).reshape(resp_rows, QH * HD)
    live = (query_positions < resp_len[0])[:, None]
    return jnp.where(live, result, 0.0).astype(jnp.bfloat16)


def solution(mesh):
    return jax.shard_map(
        per_device,
        mesh=mesh,
        in_specs=(
            P(("ctx", "vis"), None),
            P(),
            P(None, "vis"),
            P("vis", None),
            P(),
            P(None, "vis"),
            P(),
            P(),
            P("ctx", "vis"),
            P("vis"),
            P("vis", None),
            P("ctx", None),
            P("ctx", None),
            P("ctx"),
        ),
        out_specs=P("ctx", None),
        check_vma=False,
    )
```

profile of v0, /device:TPU:0, one launch (start us, length us, event | category | flops | bytes accessed | tf_op | source)
XLA Modules:
  0.0 479.5 jit_solution(3582567656449933819)
XLA Ops:
  6.5 1.2 convert_reduce_fusion
  7.8 1.2 fusion.38
  9.0 1.9 fusion.40
  11.0 0.7 all-gather.9.cloned.1.call-update
  11.8 35.8 %all-gather.7.cloned.1.call-done = bf16[1024,1280]{1,0:T(8,128)(2,1)} async-done(((bf16[128,1280]{1,0:T(8,128)(2,1)}), bf16[1024,1280]{1,0:T(8,128)(2,1)}) %all-gather.7.cloned.1.call-update) | async-done | bytes 2621456 | tf_op jit(solution)/shard_map/all_gather | solution.py:96
  47.5 3.5 convolution_convert_fusion
  51.1 1.3 copy.61
  52.4 11.1 %while.40 = (s32[]{:T(128)}, bf16[2,1024,80]{2,1,0:T(8,128)(2,1)}, bf16[2,1024,240]{2,1,0:T(8,128)(2,1)}, s32[]{:T(128)}, s32[]{:T(128)}, /*index=5*/s32[]{:T(128)}) while((s32[]{:T(128)}, bf16[2,1024,80]{2,1,0:T(8,128)(2,1)}, bf16[2,1024,240]{2,1,0:T(8,128)(2,1)}, s32[]{:T(128)}, s32[]{:T(128)}, /*index=5*/s32[]{:T(128)}) %tuple.93), condition=%wide.region_13.14_spmd, body=%wide.region_8.0_spmd.sunk | while | flops 172047360 | bytes 9758946 | solution.py:57
  52.4 1.1 dynamic-slice_bitcast_fusion.2
  53.7 3.3 while.42
  54.2 0.5 fusion.97
  54.8 0.6 fusion.98
  55.9 0.5 fusion.97
  56.4 0.6 fusion.98
  57.2 0.7 bitcast_dynamic-update-slice_fusion.2
  57.9 1.1 dynamic-slice_bitcast_fusion.2
  59.2 3.3 while.42
  60.3 0.6 fusion.98
  62.0 0.6 fusion.98
  62.8 0.7 bitcast_dynamic-update-slice_fusion.2
  63.5 1.6 copy.110
  65.1 31.0 %all_to_all.20 = bf16[1024,2,80]{2,1,0:T(2,128)(2,1)S(1)} all-to-all(bf16[1024,2,80]{2,1,0:T(2,128)(2,1)S(1)} %bitcast.150), channel_id=1, replica_groups=mesh['ctx'=4,'vis'=8] {'vis'}, dimensions={0} | all-to-all | bytes 655360 | tf_op jit(solution)/shard_map/all_to_all | solution.py:100
  96.5 2.4 all-gather.9.cloned.1.call-done
  98.9 2.7 fusion.72
  102.0 0.9 reshape.399
  103.9 31.7 %all-gather.11.cloned.1.call-done = bf16[256,5120]{1,0:T(8,128)(2,1)} async-done(((bf16[32,5120]{1,0:T(8,128)(2,1)}), bf16[256,5120]{1,0:T(8,128)(2,1)}) %all-gather.11.cloned.1.call-update) | async-done | bytes 2621456 | tf_op jit(solution)/shard_map/all_gather | solution.py:111
  135.6 7.6 %convolution_convert_fusion.1 = bf16[256,1024]{1,0:T(8,128)(2,1)S(1)} fusion(bf16[256,5120]{1,0:T(8,128)(2,1)} %all-gather.11.cloned.1.call-done, bf16[5120,1024]{1,0:T(8,128)(2,1)} %param.25), kind=kOutput, calls=%fused_computation.52 | convolution fusion | flops 2684616704 | bytes 13631488 | tf_op jit(solution)/shard_map/dot_general | solution.py:110
  143.2 2.7 gather_fusion
  145.9 2.2 select_select_fusion.1
  148.1 3.6 all-to-all-start.1
  152.2 3.7 gather_fusion.2
  155.9 3.1 scatter_custom_fusion
  159.0 4.0 all-to-all-done.1
  163.1 5.4 %gather_fusion.1 = bf16[1024,1024]{1,0:T(8,128)(2,1)} fusion(bf16[384,1024]{1,0:T(8,128)(2,1)S(1)} %bitcast.141, s32[1024]{0:T(1024)S(1)} %fusion.55), kind=kCustom, calls=%fused_computation.1 | custom fusion | bytes 4198400 | tf_op jit(solution)/shard_map/jit(_take)/gather | solution.py:139
  168.4 4.1 fusion.19
  172.5 13.9 %psum.7 = f32[1024]{0:T(1024)S(1)} all-reduce(f32[1024]{0:T(1024)S(1)} %get-tuple-element.265), channel_id=1, replica_groups=mesh['ctx'=4,'vis'=8] {'vis'}, use_global_device_ids=true, to_apply=%region_17.18 | all-reduce | flops 1024 | bytes 8192 | tf_op jit(solution)/shard_map/psum | solution.py:142
  186.4 5.9 %fusion.26 = f32[1024,1024]{1,0:T(8,128)} fusion(bf16[1024,1024]{1,0:T(8,128)(2,1)S(1)} %copy-done, bf16[1024,1024]{1,0:T(8,128)(2,1)} %get-tuple-element.266, f32[1024]{0:T(1024)S(1)} %copy-done.5, f32[1024]{0:T(1024)S(1)} %add_rsqrt_fusion), kind=kOutput, calls=%fused_computation.43 | convolution fusion | flops 2151677952 | bytes 8396800 | tf_op jit(solution)/shard_map/dot_general | solution.py:146
  192.4 47.3 %reduce-scatter.2.cloned.1.call-done = f32[128,1024]{1,0:T(8,128)} async-done(((f32[1024,1024]{1,0:T(8,128)}), f32[128,1024]{1,0:T(8,128)}) %reduce-scatter.2.cloned.1.call-update) | async-done | bytes 524304 | tf_op jit(solution)/shard_map/reduce_scatter | solution.py:145
  239.7 1.8 convert_element_type.58
  241.6 1.4 copy.86
  243.0 0.7 fusion.71
  244.3 22.3 %all-gather.13.cloned.1.call-done = bf16[512,1024]{1,0:T(8,128)(2,1)} async-done(((bf16[128,1024]{1,0:T(8,128)(2,1)}), bf16[512,1024]{1,0:T(8,128)(2,1)}) %all-gather.13.cloned.1.call-update) | async-done | bytes 1048592 | tf_op jit(solution)/shard_map/all_gather | solution.py:212
  266.6 2.3 fusion.70
  268.9 2.0 reshape.401
  270.8 5.5 %bitcast_reduce_fusion = (f32[4,8,128]{2,1,0:T(8,128)S(1)}, f32[4,512,128,8]{2,1,3,0:T(8,128)}) fusion(bf16[128,4,8,128]{3,2,1,0:T(8,128)(2,1)S(1)} %bitcast.145, bf16[512,4,128,1]{2,1,0,3:T(4,128)(2,1)} %bitcast.148), kind=kOutput, calls=%fused_computation.30 | convolution fusion | flops 541061120 | bytes 9977856 | tf_op jit(solution)/shard_map/rkgd,nkd->kgrn/dot_general | solution.py:160
  276.4 1.2 reshape.403
  277.6 5.4 %fusion.22 = f32[4,8,128,128]{3,2,1,0:T(8,128)S(1)} fusion(f32[4,512,128,8]{2,1,3,0:T(8,128)} %get-tuple-element.289, f32[4,8,128]{2,1,0:T(8,128)S(1)} %get-tuple-element.277, bf16[512,4,128,1]{2,1,0,3:T(4,128)(2,1)S(1)} %bitcast.152), kind=kOutput, calls=%fused_computation.39 | convolution fusion | flops 543162368 | bytes 11026432 | tf_op jit(solution)/shard_map/kgrn,nkd->kgrd/dot_general | solution.py:170
  283.0 2.6 multiply_add_fusion
  286.3 4.8 %fusion.18 = f32[4,8,128]{2,1,0:T(8,128)S(1)} fusion(f32[4,512,128,8]{2,1,3,0:T(8,128)} %get-tuple-element.289, f32[4,8,128]{2,1,0:T(8,128)S(1)} %get-tuple-element.277), kind=kLoop, calls=%fused_computation.33 | loop fusion | flops 6287360 | bytes 8421376 | tf_op jit(solution)/shard_map/reduce_sum | solution.py:169
  291.2 14.7 %all_gather.30 = f32[8,4,8,128]{3,2,1,0:T(8,128)S(1)} all-gather(f32[1,4,8,128]{3,2,1,0:T(8,128)S(1)} %get-tuple-element.279), channel_id=1, replica_groups=mesh['ctx'=4,'vis'=8] {'vis'}, dimensions={0}, use_global_device_ids=true | all-gather | bytes 147456 | tf_op jit(solution)/shard_map/all_gather | solution.py:19
  305.8 21.1 %all_gather.31 = f32[8,4,8,128]{3,2,1,0:T(8,128)S(1)} all-gather(f32[1,4,8,128]{3,2,1,0:T(8,128)S(1)} %get-tuple-element.278), channel_id=1, replica_groups=mesh['ctx'=4,'vis'=8] {'vis'}, dimensions={0}, use_global_device_ids=true | all-gather | bytes 147456 | tf_op jit(solution)/shard_map/all_gather | solution.py:19
  326.9 111.4 %all-gather.15.cloned.1.call-done = f32[32,8,128,128]{3,2,1,0:T(8,128)} async-done(((f32[4,8,128,128]{3,2,1,0:T(8,128)}), f32[32,8,128,128]{3,2,1,0:T(8,128)}) %all-gather.15.cloned.1.call-update) | async-done | bytes 16777232 | tf_op jit(solution)/shard_map/all_gather | solution.py:19
  438.3 3.2 slice.51
  441.5 27.0 %while.41 = (s32[]{:T(128)}, f32[4,8,128]{2,1,0:T(8,128)S(1)}, f32[4,8,128]{2,1,0:T(8,128)S(1)}, f32[4,8,128,128]{3,2,1,0:T(8,128)}, f32[8,4,8,128]{3,2,1,0:T(8,...) while((s32[]{:T(128)}, f32[4,8,128]{2,1,0:T(8,128)S(1)}, ...), condition=%wide.region_23.24_spmd, body=%wide.region_22.23_spmd.sunk | while | flops 1597445 | bytes 6455447 | solution.py:25
  441.5 3.8 fusion.93
  445.4 3.8 fusion.93
  449.2 3.8 fusion.93
  453.1 3.8 fusion.93
  457.0 3.8 fusion.93
  460.8 3.8 fusion.93
  464.7 3.8 fusion.93
  468.5 1.9 divide_bitcast_fusion
  470.5 0.7 copy.70
  471.2 1.5 fusion.28
  (84 shorter events, 7.1 us)
Async XLA Ops:
  6.5 179.9 %copy-start = (bf16[1024,1024]{1,0:T(8,128)(2,1)S(1)}, bf16[1024,1024]{1,0:T(8,128)(2,1)}, u32[]{:S(2)}) copy-start(bf16[1024,1024]{1,0:T(8,128)(2,1)} %param.30) | copy-start | bytes 6291460
  6.5 41.0 %all-gather.7.cloned.1.call-start = ((), (), s32[]{:S(2)}) async-start(), calls=%async_computation.3 | async-start | bytes 2949120 | tf_op jit(solution)/shard_map/all_gather | solution.py:96
  11.0 87.9 %all-gather.9.cloned.1.call-start = ((), (), s32[]{:S(2)}) async-start(), calls=%async_computation.4 | async-start | bytes 3686400 | tf_op jit(solution)/shard_map/all_gather | solution.py:105
  11.7 123.8 %all-gather.11.cloned.1.call-start = ((), (), s32[]{:S(2)}) async-start(), calls=%async_computation.5 | async-start | bytes 2949120 | tf_op jit(solution)/shard_map/all_gather | solution.py:111
  63.5 35.4 %copy-start.2 = (bf16[128,1280]{1,0:T(8,128)(2,1)S(1)}, bf16[128,1280]{1,0:T(8,128)(2,1)}, u32[]{:S(2)}) copy-start(bf16[128,1280]{1,0:T(8,128)(2,1)} %param.20) | copy-start | bytes 983044
  98.9 2.9 copy-start.3
  101.6 1.4 copy-start.4
  145.9 6.3 %copy-start.1 = (s32[4,256]{1,0:T(4,128)S(1)}, s32[4,256]{1,0:T(4,128)}, u32[]{:S(2)}) copy-start(s32[4,256]{1,0:T(4,128)} %param.27) | copy-start | bytes 12292
  148.1 15.0 %all-to-all-start.1 = ((bf16[4,96,1024]{2,1,0:T(8,128)(2,1)}), bf16[4,96,1024]{2,1,0:T(8,128)(2,1)S(1)}, u32[]{:S(2)}, u32[]{:S(2)}) async-start(bf16[4,96,1024]{2,1,0:T(8,128)(2,1)} %select_select_fusion.1), calls=%async_computation.1 | async-start | bytes 1572864 | tf_op jit(solution)/shard_map/all_to_all | solution.py:129
  151.8 88.0 %reduce-scatter.2.cloned.1.call-start = ((), (), s32[]{:S(2)}) async-start(), calls=%async_computation.6 | async-start | bytes 4718592 | tf_op jit(solution)/shard_map/reduce_scatter | solution.py:145
  168.4 18.0 %copy-start.5 = (f32[1024]{0:T(1024)S(1)}, f32[1024]{0:T(1024)}, u32[]{:S(2)}) copy-start(f32[1024]{0:T(1024)} %param.29) | copy-start | bytes 12292
  192.4 74.3 %all-gather.13.cloned.1.call-start = ((), (), s32[]{:S(2)}) async-start(), calls=%async_computation.7 | async-start | bytes 1310720 | tf_op jit(solution)/shard_map/all_gather | solution.py:212
  241.5 196.8 %all-gather.15.cloned.1.call-start = ((), (), s32[]{:S(2)}) async-start(), calls=%async_computation.8 | async-start | bytes 18874368 | tf_op jit(solution)/shard_map/all_gather | solution.py:19
Sparse Core Ops, SparseCore 0:
  11.1 36.4 all-gather.6
  49.2 49.6 all-gather.8
  103.1 32.4 all-gather.10
  192.5 47.1 reduce-scatter.1
  241.6 24.9 all-gather.12
  285.7 152.5 all-gather.14
where the time goes:
time: 480 us; the launch traced here: 479 us
  waiting for transfers between devices  256 us (53%)
  blocking collectives  80.7 us (17%)
  other arithmetic  51.2 us (11%)
  matrix products  38.1 us (8%)
  local copies, waits for them, and re-layouts  35.4 us (7%)
  between operations  14.4 us (3%)
    all_gather x1, waiting for transfers between devices, merged_2(): everything = jax.tree.map(lambda part: lax.all_gather(part, axis), shard)  111 us
    reduce_scatter x1, waiting for transfers between devices, per_device(): lax.psum_scatter(jnp.dot(scaled, w_kv, preferred_element_type=jnp.float32...  47.3 us
    all_gather x2, blocking collectives, merged_2(): everything = jax.tree.map(lambda part: lax.all_gather(part, axis), shard)  35.8 us
    all_gather x1, waiting for transfers between devices, per_device(): lax.all_gather(normed, 'vis', axis=0, tiled=True)  35.8 us
    all_gather x1, waiting for transfers between devices, per_device(): lax.all_gather(merged, 'vis', axis=0, tiled=True)  31.7 us
    all_to_all x1, blocking collectives, per_device(): lax.all_to_all(heads, 'vis', split_axis=0, concat_axis=1, tiled=True)  31 us
    add x7, other arithmetic, combine_partial(): first[2] * fade_one[..., None] + second[2] * fade_two[..., None]  26.9 us
    all_gather x1, waiting for transfers between devices, per_device(): lax.all_gather(kv_share, 'ctx', axis=0, tiled=True)  22.3 us
  transfers between devices with their start and end apart: 7, of which 7 were waited for; matrix products, arithmetic and copies ran while one was open for 7% of the time, Pallas kernels for 0%

commit v1 on v0

--- a/solution.py
+++ b/solution.py
@@ -13,6 +13,27 @@
 VHD = 80
 MD = 5120
 EPS = 1e-06
+
+
+def laid_out(blocks, dim):
+    blocks = jnp.moveaxis(blocks, 0, dim)
+    shape = blocks.shape
+    return blocks.reshape(*shape[:dim], shape[dim] * shape[dim + 1], *shape[dim + 2 :])
+
+
+def collected_by_bits(x, axis):
+    count, index = (lax.axis_size(axis), lax.axis_index(axis))
+    parts, bit = (x[None], 1)
+    while bit < count:
+        other = lax.ppermute(parts, axis, [(i, i ^ bit) for i in range(count)])
+        low = index & bit == 0
+        parts = jnp.concatenate([jnp.where(low, parts, other), jnp.where(low, other, parts)])
+        bit *= 2
+    return parts
+
+
+def gather_by_bits(value, axis, dim):
+    return laid_out(collected_by_bits(value, axis), dim)
 
 
 def merged_2(shard, axis, combine):
@@ -108,9 +129,7 @@
     mixed = floats + projected
     merged = layer_norm(mixed, merge_gain).astype(jnp.bfloat16).reshape(patch_count // 4, MD)
     visual = jnp.dot(
-        lax.all_gather(merged, "vis", axis=0, tiled=True),
-        w_merge,
-        preferred_element_type=jnp.float32,
+        gather_by_bits(merged, "vis", 0), w_merge, preferred_element_type=jnp.float32
     ).astype(jnp.bfloat16)
     image_tokens = visual.shape[0]
     capacity = 3 * (image_tokens // ctx_count) // 2

time: 480 us -> 529 us (1.10)
  waiting for transfers between devices: 256 us -> 301 us
    ppermute x0 -> x3, waiting for transfers between devices: none -> 76.8 us  [collected_by_bits(): other = lax.ppermute(parts, axis, [(i, i ^ bit) for i in range(count)])]
    all_gather x1 -> x0, waiting for transfers between devices: 31.7 us -> none  [per_device(): lax.all_gather(merged, 'vis', axis=0, tiled=True)]
  transfers between devices with their start and end apart: 7 -> 9, of which waited for: 7 -> 9; matrix products, arithmetic and copies ran while one was open for 7% -> 6% of each run, Pallas kernels for 0% -> 0%
where the time goes in v1:
time: 529 us; the launch traced here: 528 us
  waiting for transfers between devices  301 us (57%)
  blocking collectives  80.2 us (15%)
  other arithmetic  55.6 us (11%)
  matrix products  37.3 us (7%)
  local copies, waits for them, and re-layouts  35.2 us (7%)
  between operations  14.1 us (3%)
    all_gather x1, waiting for transfers between devices, merged_2(): everything = jax.tree.map(lambda part: lax.all_gather(part, axis), shard)  112 us
    ppermute x3, waiting for transfers between devices, collected_by_bits(): other = lax.ppermute(parts, axis, [(i, i ^ bit) for i in range(count)])  76.8 us
    reduce_scatter x1, waiting for transfers between devices, per_device(): lax.psum_scatter(jnp.dot(scaled, w_kv, preferred_element_type=jnp.float32...  47.3 us
    all_gather x1, waiting for transfers between devices, per_device(): lax.all_gather(normed, 'vis', axis=0, tiled=True)  35.8 us
    all_gather x2, blocking collectives, merged_2(): everything = jax.tree.map(lambda part: lax.all_gather(part, axis), shard)  35.6 us
    all_to_all x1, blocking collectives, per_device(): lax.all_to_all(heads, 'vis', split_axis=0, concat_axis=1, tiled=True)  31 us
    add x7, other arithmetic, combine_partial(): first[2] * fade_one[..., None] + second[2] * fade_two[..., None]  26.9 us
    all_gather x1, waiting for transfers between devices, per_device(): lax.all_gather(kv_share, 'ctx', axis=0, tiled=True)  22.3 us
  transfers between devices with their start and end apart: 9, of which 9 were waited for; matrix products, arithmetic and copies ran while one was open for 6% of the time, Pallas kernels for 0%

profile of v1, /device:TPU:0, one launch (start us, length us, event | category | flops | bytes accessed | tf_op | source)
XLA Modules:
  0.0 527.6 jit_solution(13517762090334433087)
XLA Ops:
  6.5 1.2 convert_reduce_fusion
  7.8 1.2 fusion.38
  9.0 1.9 fusion.40
  11.0 0.7 all-gather.8.cloned.1.call-update
  11.7 35.8 %all-gather.6.cloned.1.call-done = bf16[1024,1280]{1,0:T(8,128)(2,1)} async-done(((bf16[128,1280]{1,0:T(8,128)(2,1)}), bf16[1024,1280]{1,0:T(8,128)(2,1)}) %all-gather.6.cloned.1.call-update) | async-done | bytes 2621456 | tf_op jit(solution)/shard_map/all_gather | solution.py:117
  47.5 3.5 convolution_convert_fusion
  51.1 1.3 copy.61
  52.4 11.1 %while.40 = (s32[]{:T(128)}, bf16[2,1024,80]{2,1,0:T(8,128)(2,1)}, bf16[2,1024,240]{2,1,0:T(8,128)(2,1)}, s32[]{:T(128)}, s32[]{:T(128)}, /*index=5*/s32[]{:T(128)}) while((s32[]{:T(128)}, bf16[2,1024,80]{2,1,0:T(8,128)(2,1)}, bf16[2,1024,240]{2,1,0:T(8,128)(2,1)}, s32[]{:T(128)}, s32[]{:T(128)}, /*index=5*/s32[]{:T(128)}) %tuple.96), condition=%wide.region_13.14_spmd, body=%wide.region_8.0_spmd.sunk | while | flops 172047360 | bytes 9758946 | solution.py:78
  52.4 1.1 dynamic-slice_bitcast_fusion.2
  53.7 3.3 while.42
  56.4 0.6 fusion.98
  57.2 0.7 bitcast_dynamic-update-slice_fusion.2
  57.9 1.1 dynamic-slice_bitcast_fusion.2
  59.2 3.3 while.42
  62.8 0.7 bitcast_dynamic-update-slice_fusion.2
  63.5 1.6 copy.110
  65.1 31.0 %all_to_all.20 = bf16[1024,2,80]{2,1,0:T(2,128)(2,1)S(1)} all-to-all(bf16[1024,2,80]{2,1,0:T(2,128)(2,1)S(1)} %bitcast.152), channel_id=1, replica_groups=mesh['ctx'=4,'vis'=8] {'vis'}, dimensions={0} | all-to-all | bytes 655360 | tf_op jit(solution)/shard_map/all_to_all | solution.py:121
  96.5 2.4 all-gather.8.cloned.1.call-done
  98.9 2.7 fusion.72
  102.5 1.4 collective-permute-done
  104.0 0.7 copy-done.3
  105.2 16.6 %collective-permute-done.1 = bf16[2,32,5120]{2,1,0:T(8,128)(2,1)} collective-permute-done((bf16[2,32,5120]{2,1,0:T(8,128)(2,1)S(1)}, bf16[2,32,5120]{2,1,0:T(8,128)(2,1)}, u32[]{:S(2)}, u32[]{:S(2)}) %collective-permute-start.1) | collective-permute-done | bytes 655392 | tf_op jit(solution)/shard_map/ppermute | solution.py:28
  121.8 1.4 broadcast_select_fusion.3
  123.1 1.2 pad_maximum_fusion.1
  124.9 58.8 %collective-permute-done.2 = bf16[4,32,5120]{2,1,0:T(8,128)(2,1)} collective-permute-done((bf16[4,32,5120]{2,1,0:T(8,128)(2,1)}, bf16[4,32,5120]{2,1,0:T(8,128)(2,1)}, u32[]{:S(2)}, u32[]{:S(2)}) %collective-permute-start.2) | collective-permute-done | bytes 1310752 | tf_op jit(solution)/shard_map/ppermute | solution.py:28
  183.7 1.5 broadcast_select_fusion.1
  185.4 6.8 %convolution_convert_fusion.1 = bf16[256,1024]{1,0:T(8,128)(2,1)S(1)} fusion(bf16[256,5120]{1,0:T(8,128)(2,1)S(1)} %bitcast.151, bf16[5120,1024]{1,0:T(8,128)(2,1)} %param.25), kind=kOutput, calls=%fused_computation.56 | convolution fusion | flops 2684616704 | bytes 13631488 | tf_op jit(solution)/shard_map/dot_general | solution.py:131
  192.2 2.7 gather_fusion
  194.9 2.2 select_select_fusion.1
  197.1 3.7 all-to-all-start.1
  201.3 3.7 gather_fusion.2
  205.0 2.9 scatter_custom_fusion
  208.0 3.9 all-to-all-done.1
  211.9 5.4 %gather_fusion.1 = bf16[1024,1024]{1,0:T(8,128)(2,1)} fusion(bf16[384,1024]{1,0:T(8,128)(2,1)S(1)} %bitcast.142, s32[1024]{0:T(1024)S(1)} %fusion.55), kind=kCustom, calls=%fused_computation.1 | custom fusion | bytes 4198400 | tf_op jit(solution)/shard_map/jit(_take)/gather | solution.py:158
  217.3 4.1 fusion.19
  221.3 13.6 %psum.7 = f32[1024]{0:T(1024)S(1)} all-reduce(f32[1024]{0:T(1024)S(1)} %get-tuple-element.265), channel_id=1, replica_groups=mesh['ctx'=4,'vis'=8] {'vis'}, use_global_device_ids=true, to_apply=%region_17.18 | all-reduce | flops 1024 | bytes 8192 | tf_op jit(solution)/shard_map/psum | solution.py:161
  234.9 5.9 %fusion.26 = f32[1024,1024]{1,0:T(8,128)} fusion(bf16[1024,1024]{1,0:T(8,128)(2,1)S(1)} %copy-done, bf16[1024,1024]{1,0:T(8,128)(2,1)} %get-tuple-element.266, f32[1024]{0:T(1024)S(1)} %copy-done.7, f32[1024]{0:T(1024)S(1)} %add_rsqrt_fusion), kind=kOutput, calls=%fused_computation.44 | convolution fusion | flops 2151677952 | bytes 8396800 | tf_op jit(solution)/shard_map/dot_general | solution.py:165
  240.9 47.3 %reduce-scatter.2.cloned.1.call-done = f32[128,1024]{1,0:T(8,128)} async-done(((f32[1024,1024]{1,0:T(8,128)}), f32[128,1024]{1,0:T(8,128)}) %reduce-scatter.2.cloned.1.call-update) | async-done | bytes 524304 | tf_op jit(solution)/shard_map/reduce_scatter | solution.py:164
  288.2 1.8 convert_element_type.58
  290.0 1.4 copy.86
  291.5 0.7 fusion.71
  292.8 22.3 %all-gather.10.cloned.1.call-done = bf16[512,1024]{1,0:T(8,128)(2,1)} async-done(((bf16[128,1024]{1,0:T(8,128)(2,1)}), bf16[512,1024]{1,0:T(8,128)(2,1)}) %all-gather.10.cloned.1.call-update) | async-done | bytes 1048592 | tf_op jit(solution)/shard_map/all_gather | solution.py:231
  315.1 2.3 fusion.70
  317.3 2.0 reshape.401
  319.3 5.5 %bitcast_reduce_fusion = (f32[4,8,128]{2,1,0:T(8,128)S(1)}, f32[4,512,128,8]{2,1,3,0:T(8,128)}) fusion(bf16[128,4,8,128]{3,2,1,0:T(8,128)(2,1)S(1)} %bitcast.146, bf16[512,4,128,1]{2,1,0,3:T(4,128)(2,1)} %bitcast.149), kind=kOutput, calls=%fused_computation.30 | convolution fusion | flops 541061120 | bytes 9977856 | tf_op jit(solution)/shard_map/rkgd,nkd->kgrn/dot_general | solution.py:179
  324.8 1.2 reshape.403
  326.0 5.4 %fusion.22 = f32[4,8,128,128]{3,2,1,0:T(8,128)S(1)} fusion(f32[4,512,128,8]{2,1,3,0:T(8,128)} %get-tuple-element.295, f32[4,8,128]{2,1,0:T(8,128)S(1)} %get-tuple-element.283, bf16[512,4,128,1]{2,1,0,3:T(4,128)(2,1)S(1)} %bitcast.154), kind=kOutput, calls=%fused_computation.39 | convolution fusion | flops 543162368 | bytes 11026432 | tf_op jit(solution)/shard_map/kgrn,nkd->kgrd/dot_general | solution.py:189
  331.4 2.6 multiply_add_fusion
  334.8 4.8 fusion.18
  339.6 14.9 %all_gather.26 = f32[8,4,8,128]{3,2,1,0:T(8,128)S(1)} all-gather(f32[1,4,8,128]{3,2,1,0:T(8,128)S(1)} %get-tuple-element.285), channel_id=1, replica_groups=mesh['ctx'=4,'vis'=8] {'vis'}, dimensions={0}, use_global_device_ids=true | all-gather | bytes 147456 | tf_op jit(solution)/shard_map/all_gather | solution.py:40
  354.5 20.7 %all_gather.27 = f32[8,4,8,128]{3,2,1,0:T(8,128)S(1)} all-gather(f32[1,4,8,128]{3,2,1,0:T(8,128)S(1)} %get-tuple-element.284), channel_id=1, replica_groups=mesh['ctx'=4,'vis'=8] {'vis'}, dimensions={0}, use_global_device_ids=true | all-gather | bytes 147456 | tf_op jit(solution)/shard_map/all_gather | solution.py:40
  375.2 111.6 %all-gather.12.cloned.1.call-done = f32[32,8,128,128]{3,2,1,0:T(8,128)} async-done(((f32[4,8,128,128]{3,2,1,0:T(8,128)}), f32[32,8,128,128]{3,2,1,0:T(8,128)}) %all-gather.12.cloned.1.call-update) | async-done | bytes 16777232 | tf_op jit(solution)/shard_map/all_gather | solution.py:40
  486.8 3.2 slice.51
  489.9 27.0 %while.41 = (s32[]{:T(128)}, f32[4,8,128]{2,1,0:T(8,128)S(1)}, f32[4,8,128]{2,1,0:T(8,128)S(1)}, f32[4,8,128,128]{3,2,1,0:T(8,128)}, f32[8,4,8,128]{3,2,1,0:T(8,...) while((s32[]{:T(128)}, f32[4,8,128]{2,1,0:T(8,128)S(1)}, ...), condition=%wide.region_23.24_spmd, body=%wide.region_22.23_spmd.sunk | while | flops 1597445 | bytes 6455447 | solution.py:46
  490.0 3.8 fusion.93
  493.8 3.8 fusion.93
  497.7 3.8 fusion.93
  501.5 3.8 fusion.93
  505.4 3.8 fusion.93
  509.3 3.8 fusion.93
  513.1 3.8 fusion.93
  517.0 1.9 divide_bitcast_fusion
  518.9 0.7 copy.70
  519.6 1.5 fusion.28
  (97 shorter events, 10.9 us)
Async XLA Ops:
  6.5 228.4 %copy-start = (bf16[1024,1024]{1,0:T(8,128)(2,1)S(1)}, bf16[1024,1024]{1,0:T(8,128)(2,1)}, u32[]{:S(2)}) copy-start(bf16[1024,1024]{1,0:T(8,128)(2,1)} %param.30) | copy-start | bytes 6291460
  6.5 41.0 %all-gather.6.cloned.1.call-start = ((), (), s32[]{:S(2)}) async-start(), calls=%async_computation.3 | async-start | bytes 2949120 | tf_op jit(solution)/shard_map/all_gather | solution.py:117
  11.0 87.9 %all-gather.8.cloned.1.call-start = ((), (), s32[]{:S(2)}) async-start(), calls=%async_computation.4 | async-start | bytes 3686400 | tf_op jit(solution)/shard_map/all_gather | solution.py:126
  63.5 35.4 %copy-start.2 = (bf16[128,1280]{1,0:T(8,128)(2,1)S(1)}, bf16[128,1280]{1,0:T(8,128)(2,1)}, u32[]{:S(2)}) copy-start(bf16[128,1280]{1,0:T(8,128)(2,1)} %param.20) | copy-start | bytes 983044
  98.9 2.9 copy-start.5
  101.8 3.0 copy-start.6
  102.2 1.7 collective-permute-start
  103.9 0.7 copy-start.3
  104.0 0.8 copy-start.4
  104.8 17.0 %collective-permute-start.1 = (bf16[2,32,5120]{2,1,0:T(8,128)(2,1)S(1)}, bf16[2,32,5120]{2,1,0:T(8,128)(2,1)}, u32[]{:S(2)}, u32[]{:S(2)}) collective-permute-start(bf16[2,32,5120]{2,1,0:T(8,128)(2,1)S(1)} %pad_maximum_fusion.2), channel_id=1, source_target_pairs={{0,2},{1,3},{2,0},{3,1},{4,6},{5,7},{6,4},{7,5},{8,10},{9,11},{10,... | collective-permute-start | bytes 1966088 | tf_op jit(solution)/shard_map/ppermute | solution.py:28
  124.3 59.3 %collective-permute-start.2 = (bf16[4,32,5120]{2,1,0:T(8,128)(2,1)}, bf16[4,32,5120]{2,1,0:T(8,128)(2,1)}, u32[]{:S(2)}, u32[]{:S(2)}) collective-permute-start(bf16[4,32,5120]{2,1,0:T(8,128)(2,1)} %pad_maximum_fusion.1), channel_id=1, source_target_pairs={{0,4},{1,5},{2,6},{3,7},{4,0},{5,1},{6,2},{7,3},{8,12},{9,13},{10,... | collective-permute-start | bytes 3932168 | tf_op jit(solution)/shard_map/ppermute | solution.py:28
  194.9 6.4 %copy-start.1 = (s32[4,256]{1,0:T(4,128)S(1)}, s32[4,256]{1,0:T(4,128)}, u32[]{:S(2)}) copy-start(s32[4,256]{1,0:T(4,128)} %param.27) | copy-start | bytes 12292
  197.1 14.7 %all-to-all-start.1 = ((bf16[4,96,1024]{2,1,0:T(8,128)(2,1)}), bf16[4,96,1024]{2,1,0:T(8,128)(2,1)S(1)}, u32[]{:S(2)}, u32[]{:S(2)}) async-start(bf16[4,96,1024]{2,1,0:T(8,128)(2,1)} %select_select_fusion.1), calls=%async_computation.1 | async-start | bytes 1572864 | tf_op jit(solution)/shard_map/all_to_all | solution.py:148
  200.8 87.4 %reduce-scatter.2.cloned.1.call-start = ((), (), s32[]{:S(2)}) async-start(), calls=%async_computation.5 | async-start | bytes 4718592 | tf_op jit(solution)/shard_map/reduce_scatter | solution.py:164
  217.3 17.7 %copy-start.7 = (f32[1024]{0:T(1024)S(1)}, f32[1024]{0:T(1024)}, u32[]{:S(2)}) copy-start(f32[1024]{0:T(1024)} %param.29) | copy-start | bytes 12292
  240.8 74.2 %all-gather.10.cloned.1.call-start = ((), (), s32[]{:S(2)}) async-start(), calls=%async_computation.6 | async-start | bytes 1310720 | tf_op jit(solution)/shard_map/all_gather | solution.py:231
  290.0 196.8 %all-gather.12.cloned.1.call-start = ((), (), s32[]{:S(2)}) async-start(), calls=%async_computation.7 | async-start | bytes 18874368 | tf_op jit(solution)/shard_map/all_gather | solution.py:40
Sparse Core Ops, SparseCore 0:
  11.1 36.4 all-gather.5
  49.2 49.6 all-gather.7
  241.0 47.1 reduce-scatter.1
  290.1 24.9 all-gather.9
  334.1 152.5 all-gather.11
